TPU v7x, 512 devices: a whole 4x8x8 slice. The times are simulated.
512 devices in a mesh: dp: 32 (over y, x), seq: 16 (over z, core).
Axes of the slice: x: 4, y: 8, z: 8, core: 2. Of those that a mesh axis runs over, the one named last changes fastest.
Arguments:
- queries: bfloat16 [32, 2048, 2048], P('dp', 'seq'), may hold values from -6 to 6
- keys_in: bfloat16 [32, 2048, 2048], P('dp', 'seq'), may hold values from -6 to 6
- values_in: bfloat16 [32, 2048, 2048], P('dp', 'seq'), may hold values from -6 to 6
- grad_out: bfloat16 [32, 2048, 2048], P('dp', 'seq'), may hold values from -6 to 6
- feat_w: bfloat16 [2, 16, 128, 128], replicated, may hold values from -0.5 to 0.5
Outputs:
- grad_queries: bfloat16 [32, 2048, 2048], P('dp', 'seq')
- grad_keys: bfloat16 [32, 2048, 2048], P('dp', 'seq')
- grad_values: bfloat16 [32, 2048, 2048], P('dp', 'seq')
- grad_feat: float32 [4096, 128], P('dp')
All inputs are finite; a program needn't handle non-finite values.
Results may differ from a plain program's by a relative error of at most 0.0064.
Values sent between devices are 32-bit elements; how exact they have to be, the bound alone decides.
A program may use at most 128 MiB of HBM per device.

v0:
```python
import math
import jax
import jax.numpy as jnp
from jax import lax
from jax.sharding import PartitionSpec as P


def carried_in(value, axis, join, neutral, backward):
    count, mine = (lax.axis_size(axis), lax.axis_index(axis))
    pieces = lax.all_gather(value, axis)
    if backward:
        pieces = pieces[::-1]
        mine = count - 1 - mine
    running = jnp.full_like(value, 0) + jnp.asarray(neutral, value.dtype)

    def lap(position, running):
        longer = join(running, pieces[position])
        return jnp.where(position < mine, longer, running)

    return lax.fori_loop(0, count - 1, lap, running)


def add_one(earlier, later):
    return earlier + later


def body(queries, keys_in, values_in, grad_out, feat_w):
    seq_count = lax.axis_size("seq")
    rep_count = lax.axis_size("dp")
    rows = queries.shape[1]
    heads = feat_w.shape[1]
    hsize = feat_w.shape[2]
    scale = 1.0 / math.sqrt(hsize * rows * seq_count)
    gscale = 1.0 / math.sqrt(rows * seq_count * rep_count)
    shape = (rows, heads, hsize)
    q_heads = queries[0].reshape(shape)
    k_heads = keys_in[0].reshape(shape)
    v_heads = values_in[0].reshape(shape)
    g_heads = grad_out[0].reshape(shape)
    f32 = jnp.float32
    bf16 = jnp.bfloat16
    feat_q = jnp.einsum("tha,hab->thb", q_heads, feat_w[0], preferred_element_type=f32).astype(bf16)
    feat_k = jnp.einsum("tha,hab->thb", k_heads, feat_w[1], preferred_element_type=f32).astype(bf16)
    sterm = jnp.einsum("tha,thb->hab", feat_k, v_heads, preferred_element_type=f32)
    gterm = jnp.einsum("tha,thb->hab", feat_q, g_heads, preferred_element_type=f32)
    zeros = jnp.zeros(sterm.shape, f32)
    prefix = carried_in(sterm, "seq", add_one, zeros, False)
    suffix = carried_in(gterm, "seq", add_one, zeros, True)
    causal = jnp.tril(jnp.ones((rows, rows), dtype=bool))
    p_mat = jnp.where(
        causal, scale * jnp.einsum("tha,sha->hts", feat_q, feat_k, preferred_element_type=f32), 0.0
    ).astype(bf16)
    q_mat = jnp.where(
        causal,
        scale * jnp.einsum("tha,sha->hts", g_heads, v_heads, preferred_element_type=f32),
        0.0,
    ).astype(bf16)
    state_b = prefix.astype(bf16)
    grad_b = suffix.astype(bf16)
    d_featq = (
        scale * jnp.einsum("thb,hab->tha", g_heads, state_b, preferred_element_type=f32)
        + jnp.einsum("hts,sha->tha", q_mat, feat_k, preferred_element_type=f32)
    ).astype(bf16)
    d_featk = (
        scale * jnp.einsum("thb,hab->tha", v_heads, grad_b, preferred_element_type=f32)
        + jnp.einsum("hts,tha->sha", q_mat, feat_q, preferred_element_type=f32)
    ).astype(bf16)
    d_values = (
        scale * jnp.einsum("tha,hab->thb", feat_k, grad_b, preferred_element_type=f32)
        + jnp.einsum("hts,thb->shb", p_mat, g_heads, preferred_element_type=f32)
    ).astype(bf16)
    d_queries = jnp.einsum("thb,hab->tha", d_featq, feat_w[0], preferred_element_type=f32).astype(
        bf16
    )
    d_keys = jnp.einsum("thb,hab->tha", d_featk, feat_w[1], preferred_element_type=f32).astype(bf16)
    wgrad_q = jnp.einsum("tha,thb->hab", q_heads, d_featq, preferred_element_type=f32)
    wgrad_k = jnp.einsum("tha,thb->hab", k_heads, d_featk, preferred_element_type=f32)
    local_grad = jnp.stack([wgrad_q, wgrad_k]).reshape(2 * heads * hsize, hsize)
    seq_total = lax.psum(local_grad, "seq")
    owned = lax.psum_scatter(seq_total, "dp", scatter_dimension=0, tiled=True)
    flat = (1, rows, heads * hsize)
    return (d_queries.reshape(flat), d_keys.reshape(flat), d_values.reshape(flat), owned * gscale)


def solution(mesh):
    return jax.shard_map(
        body,
        mesh=mesh,
        in_specs=(
            P("dp", "seq", None),
            P("dp", "seq", None),
            P("dp", "seq", None),
            P("dp", "seq", None),
            P(),
        ),
        out_specs=(P("dp", "seq", None), P("dp", "seq", None), P("dp", "seq", None), P("dp", None)),
        check_vma=False,
    )
```

profile of v0, /device:TPU:1, one launch (start us, length us, event | category | flops | bytes accessed | tf_op | source)
XLA Modules:
  0.0 593.4 jit_solution(17331871863249463423)
XLA Ops:
  18.7 2.4 fusion.5
  21.1 96.6 %all-gather.5.cloned.1.call-done = f32[256,128,128]{2,1,0:T(8,128)} async-done(((f32[16,128,128]{2,1,0:T(8,128)}), f32[256,128,128]{2,1,0:T(8,128)}) %all-gather.5.cloned.1.call-update) | async-done | bytes 16777232 | tf_op jit(solution)/shard_map/all_gather | solution.py:10
  117.7 24.4 %while.28 = (s32[]{:T(128)}, f32[16,128,128]{2,1,0:T(8,128)S(1)}, s32[]{:T(128)}, f32[16,16,128,128]{3,2,1,0:T(8,128)}, s32[]{:T(128)}, /*index=5*/s32[]{:T(128)}) while((s32[]{:T(128)}, f32[16,128,128]{2,1,0:T(8,128)S(1)}, s32[]{:T(128)}, f32[16,16,128,128]{3,2,1,0:T(8,128)}, s32[]{:T(128)}, /*index=5*/s32[]{:T(128)}) %tuple.79), condition=%wide.region_1.2_spmd.clone, body=%wide.region_0.1_spmd.clone.sunk | while | flops 786436 | bytes 3145821 | solution.py:20
  119.3 1.6 add_select_fusion.4
  122.6 1.6 add_select_fusion.4
  125.8 1.6 add_select_fusion.4
  129.0 1.6 add_select_fusion.4
  130.6 1.7 add_select_fusion.4
  134.0 1.6 add_select_fusion.4
  137.2 1.6 add_select_fusion.4
  138.8 1.7 add_select_fusion.4
  140.5 1.6 add_select_fusion.4
  144.0 2.5 convolution_bitcast_fusion.2
  146.5 70.1 %all-gather.7.cloned.1.call-done = f32[256,128,128]{2,1,0:T(8,128)} async-done(((f32[16,128,128]{2,1,0:T(8,128)}), f32[256,128,128]{2,1,0:T(8,128)}) %all-gather.7.cloned.1.call-update) | async-done | bytes 16777232 | tf_op jit(solution)/shard_map/all_gather | solution.py:10
  216.6 11.6 %rev.3 = f32[16,16,128,128]{3,2,1,0:T(8,128)} reverse(f32[16,16,128,128]{3,2,1,0:T(8,128)} %bitcast.81), dimensions={0} | reverse | bytes 33554432 | tf_op jit(solution)/shard_map/rev | solution.py:12
  228.3 24.2 %while.29 = (s32[]{:T(128)}, f32[16,128,128]{2,1,0:T(8,128)S(1)}, s32[]{:T(128)}, f32[16,16,128,128]{3,2,1,0:T(8,128)}, s32[]{:T(128)}, /*index=5*/s32[]{:T(128)}) while((s32[]{:T(128)}, f32[16,128,128]{2,1,0:T(8,128)S(1)}, s32[]{:T(128)}, f32[16,16,128,128]{3,2,1,0:T(8,128)}, s32[]{:T(128)}, /*index=5*/s32[]{:T(128)}) %tuple.68), condition=%wide.region_3.4_spmd.clone, body=%wide.region_2.3_spmd.clone.sunk | while | flops 786436 | bytes 3145821 | solution.py:20
  228.3 1.6 add_select_fusion.5
  229.9 1.6 add_select_fusion.5
  257.7 2.8 pad_maximum_fusion
  260.6 2.1 convolution_convert_fusion.1
  264.0 1.7 fusion.8
  265.7 208.6 %reduce-scatter.2.cloned.1.call-done = f32[128,128]{1,0:T(8,128)} async-done(((f32[4096,128]{1,0:T(8,128)}), f32[128,128]{1,0:T(8,128)}) %reduce-scatter.2.cloned.1.call-update) | async-done | bytes 65552 | tf_op jit(solution)/shard_map/reduce_scatter | solution.py:80
  476.9 2.0 copy.52
  479.9 105.5 %all-reduce.2.cloned.1.call-done = f32[128,128]{1,0:T(8,128)} async-done(((f32[128,128]{1,0:T(8,128)}), f32[128,128]{1,0:T(8,128)}) %all-reduce.2.cloned.1.call-update) | async-done | bytes 65552 | tf_op jit(solution)/shard_map/psum | solution.py:79
  (60 shorter events, 55.0 us)
Async XLA Ops:
  7.2 110.5 %all-gather.5.cloned.1.call-start = ((), (), s32[]{:S(2)}) async-start(), calls=%async_computation.1 | async-start | bytes 17825792 | tf_op jit(solution)/shard_map/all_gather | solution.py:10
  8.5 4.3 copy-start.3
  9.9 5.6 copy-start.4
  12.8 203.8 %all-gather.7.cloned.1.call-start = ((), (), s32[]{:S(2)}) async-start(), calls=%async_computation.2 | async-start | bytes 17825792 | tf_op jit(solution)/shard_map/all_gather | solution.py:10
  15.5 3.2 copy-start.5
  17.1 1.6 copy-start
  18.6 455.7 %reduce-scatter.2.cloned.1.call-start = ((), (), s32[]{:S(2)}) async-start(), calls=%async_computation.3 | async-start | bytes 2162688 | tf_op jit(solution)/shard_map/reduce_scatter | solution.py:80
  228.3 25.8 %copy-start.1 = (bf16[128,16,128]{0,2,1:T(8,128)(2,1)S(1)}, bf16[128,16,128]{0,2,1:T(8,128)(2,1)}, u32[]{:S(2)}) copy-start(bf16[128,16,128]{0,2,1:T(8,128)(2,1)} %copy-done) | copy-start | bytes 1572868
  255.4 0.8 copy-start.2
  260.5 324.9 %all-reduce.2.cloned.1.call-start = ((), (), s32[]{:S(2)}) async-start(), calls=%async_computation.4 | async-start | bytes 131072 | tf_op jit(solution)/shard_map/psum | solution.py:79
Sparse Core Ops, SparseCore 0:
  12.9 104.7 all-gather.4
  119.8 96.7 all-gather.6
  260.6 213.6 reduce-scatter.1
  476.6 108.7 all-reduce.1
where the time goes:
time: 595 us; the launch traced here: 593 us
  waiting for transfers between devices  481 us (81%)
  other arithmetic  52.2 us (9%)
  matrix products  23.7 us (4%)
  local copies, waits for them, and re-layouts  21.8 us (4%)
  between operations  14 us (2%)
    reduce_scatter x1, waiting for transfers between devices, body(): owned = lax.psum_scatter(seq_total, 'dp', scatter_dimension=0, tiled=True)  209 us
    all_gather x2, waiting for transfers between devices, carried_in(): pieces = lax.all_gather(value, axis)  167 us
    psum x1, waiting for transfers between devices, body(): seq_total = lax.psum(local_grad, 'seq')  105 us
    select_n x30, other arithmetic, lap(): return jnp.where(position < mine, longer, running)  48 us
  transfers between devices with their start and end apart: 4, of which 4 were waited for; matrix products, arithmetic and copies ran while one was open for 8% of the time, Pallas kernels for 0%

commit v1 on v0

--- a/solution.py
+++ b/solution.py
@@ -76,7 +76,11 @@
     wgrad_q = jnp.einsum("tha,thb->hab", q_heads, d_featq, preferred_element_type=f32)
     wgrad_k = jnp.einsum("tha,thb->hab", k_heads, d_featk, preferred_element_type=f32)
     local_grad = jnp.stack([wgrad_q, wgrad_k]).reshape(2 * heads * hsize, hsize)
-    seq_total = lax.psum(local_grad, "seq")
+    seq_total = local_grad
+    for hop in (1, 2, 4, 8):
+        seq_total = seq_total + lax.ppermute(
+            seq_total, "seq", [(dev, dev ^ hop) for dev in range(16)]
+        )
     owned = lax.psum_scatter(seq_total, "dp", scatter_dimension=0, tiled=True)
     flat = (1, rows, heads * hsize)
     return (d_queries.reshape(flat), d_keys.reshape(flat), d_values.reshape(flat), owned * gscale)

time: 595 us -> 733 us (1.23)
  waiting for transfers between devices: 481 us -> 614 us
  starting transfers between devices: 0.16 us -> 10.9 us
  matrix products: 23.7 us -> 15 us
    ppermute x0 -> x4, waiting for transfers between devices: none -> 236 us  [body(): lax.ppermute(seq_total, 'seq', [(dev, dev ^ hop) for dev in range(16)])]
    psum x1 -> x0, waiting for transfers between devices: 105 us -> none  [body(): seq_total = lax.psum(local_grad, 'seq')]
    ppermute x0 -> x4, starting transfers between devices: none -> 10.8 us  [body(): lax.ppermute(seq_total, 'seq', [(dev, dev ^ hop) for dev in range(16)])]
  transfers between devices with their start and end apart: 4 -> 7, of which waited for: 4 -> 7; matrix products, arithmetic and copies ran while one was open for 8% -> 5% of each run, Pallas kernels for 0% -> 0%
where the time goes in v1:
time: 733 us; the launch traced here: 728 us
  waiting for transfers between devices  614 us (84%)
  other arithmetic  51.8 us (7%)
  local copies, waits for them, and re-layouts  21.8 us (3%)
  matrix products  15 us (2%)
  between operations  14.1 us (2%)
  starting transfers between devices  10.9 us (1%)
    ppermute x4, waiting for transfers between devices, body(): lax.ppermute(seq_total, 'seq', [(dev, dev ^ hop) for dev in range(16)])  236 us
    reduce_scatter x1, waiting for transfers between devices, body(): owned = lax.psum_scatter(seq_total, 'dp', scatter_dimension=0, tiled=True)  207 us
    all_gather x2, waiting for transfers between devices, carried_in(): pieces = lax.all_gather(value, axis)  171 us
    select_n x30, other arithmetic, lap(): return jnp.where(position < mine, longer, running)  47.9 us
  transfers between devices with their start and end apart: 7, of which 7 were waited for; matrix products, arithmetic and copies ran while one was open for 5% of the time, Pallas kernels for 0%

profile of v1, /device:TPU:1, one launch (start us, length us, event | category | flops | bytes accessed | tf_op | source)
XLA Modules:
  0.0 727.8 jit_solution(15631212101687845351)
XLA Ops:
  15.5 2.4 fusion.5
  17.8 99.2 %all-gather.5.cloned.1.call-done = f32[256,128,128]{2,1,0:T(8,128)} async-done(((f32[16,128,128]{2,1,0:T(8,128)}), f32[256,128,128]{2,1,0:T(8,128)}) %all-gather.5.cloned.1.call-update) | async-done | bytes 16777232 | tf_op jit(solution)/shard_map/all_gather | solution.py:10
  117.0 24.4 %while.28 = (s32[]{:T(128)}, f32[16,128,128]{2,1,0:T(8,128)S(1)}, s32[]{:T(128)}, f32[16,16,128,128]{3,2,1,0:T(8,128)}, s32[]{:T(128)}, /*index=5*/s32[]{:T(128)}) while((s32[]{:T(128)}, f32[16,128,128]{2,1,0:T(8,128)S(1)}, s32[]{:T(128)}, f32[16,16,128,128]{3,2,1,0:T(8,128)}, s32[]{:T(128)}, /*index=5*/s32[]{:T(128)}) %tuple.77), condition=%wide.region_1.2_spmd.clone, body=%wide.region_0.1_spmd.clone.sunk | while | flops 786436 | bytes 3145821 | solution.py:20
  118.6 1.6 add_select_fusion.4
  121.8 1.6 add_select_fusion.4
  123.4 1.6 add_select_fusion.4
  125.1 1.6 add_select_fusion.4
  129.9 1.7 add_select_fusion.4
  138.1 1.7 add_select_fusion.4
  144.4 71.5 %all-gather.7.cloned.1.call-done = f32[256,128,128]{2,1,0:T(8,128)} async-done(((f32[16,128,128]{2,1,0:T(8,128)}), f32[256,128,128]{2,1,0:T(8,128)}) %all-gather.7.cloned.1.call-update) | async-done | bytes 16777232 | tf_op jit(solution)/shard_map/all_gather | solution.py:10
  215.9 11.6 %rev.3 = f32[16,16,128,128]{3,2,1,0:T(8,128)} reverse(f32[16,16,128,128]{3,2,1,0:T(8,128)} %bitcast.82), dimensions={0} | reverse | bytes 33554432 | tf_op jit(solution)/shard_map/rev | solution.py:12
  227.6 24.2 %while.29 = (s32[]{:T(128)}, f32[16,128,128]{2,1,0:T(8,128)S(1)}, s32[]{:T(128)}, f32[16,16,128,128]{3,2,1,0:T(8,128)}, s32[]{:T(128)}, /*index=5*/s32[]{:T(128)}) while((s32[]{:T(128)}, f32[16,128,128]{2,1,0:T(8,128)S(1)}, s32[]{:T(128)}, f32[16,16,128,128]{3,2,1,0:T(8,128)}, s32[]{:T(128)}, /*index=5*/s32[]{:T(128)}) %tuple.68), condition=%wide.region_3.4_spmd.clone, body=%wide.region_2.3_spmd.clone.sunk | while | flops 786436 | bytes 3145821 | solution.py:20
  251.8 1.6 convolution_multiply_fusion.2
  255.3 2.2 collective-permute-start
  257.4 3.9 collective-permute-done
  261.5 1.9 collective-permute-start.1
  263.5 46.9 %collective-permute-done.1 = f32[4096,128]{1,0:T(8,128)S(1)} collective-permute-done((f32[4096,128]{1,0:T(8,128)S(1)}, f32[4096,128]{1,0:T(8,128)S(1)}, u32[]{:S(2)}, u32[]{:S(2)}) %collective-permute-start.1) | collective-permute-done | bytes 2097184 | tf_op jit(solution)/shard_map/ppermute | solution.py:81
  310.6 3.3 collective-permute-start.2
  313.9 91.9 %collective-permute-done.2 = f32[4096,128]{1,0:T(8,128)S(1)} collective-permute-done((f32[4096,128]{1,0:T(8,128)S(1)}, f32[4096,128]{1,0:T(8,128)S(1)}, u32[]{:S(2)}, u32[]{:S(2)}) %collective-permute-start.2) | collective-permute-done | bytes 2097184 | tf_op jit(solution)/shard_map/ppermute | solution.py:81
  406.1 3.4 collective-permute-start.3
  409.5 93.6 %collective-permute-done.3 = f32[4096,128]{1,0:T(8,128)S(1)} collective-permute-done((f32[4096,128]{1,0:T(8,128)S(1)}, f32[4096,128]{1,0:T(8,128)S(1)}, u32[]{:S(2)}, u32[]{:S(2)}) %collective-permute-start.3) | collective-permute-done | bytes 2097184 | tf_op jit(solution)/shard_map/ppermute | solution.py:81
  506.0 2.6 fusion.8
  508.6 2.1 copy.54
  513.3 206.5 %reduce-scatter.2.cloned.1.call-done = f32[128,128]{1,0:T(8,128)} async-done(((f32[4096,128]{1,0:T(8,128)}), f32[128,128]{1,0:T(8,128)}) %reduce-scatter.2.cloned.1.call-update) | async-done | bytes 65552 | tf_op jit(solution)/shard_map/reduce_scatter | solution.py:84
  (89 shorter events, 58.6 us)
Async XLA Ops:
  7.2 2.8 copy-start.9
  7.2 109.8 %all-gather.5.cloned.1.call-start = ((), (), s32[]{:S(2)}) async-start(), calls=%async_computation.2 | async-start | bytes 17825792 | tf_op jit(solution)/shard_map/all_gather | solution.py:10
  8.6 3.4 copy-start.4
  10.0 0.8 copy-start.6
  10.0 2.1 copy-start.14
  10.8 1.7 copy-start.15
  12.1 203.8 %all-gather.7.cloned.1.call-start = ((), (), s32[]{:S(2)}) async-start(), calls=%async_computation.3 | async-start | bytes 17825792 | tf_op jit(solution)/shard_map/all_gather | solution.py:10
  12.7 2.7 copy-start.7
  13.1 0.8 copy-start
  15.4 704.4 %reduce-scatter.2.cloned.1.call-start = ((), (), s32[]{:S(2)}) async-start(), calls=%async_computation.1 | async-start | bytes 2162688 | tf_op jit(solution)/shard_map/reduce_scatter | solution.py:84
  141.4 1.1 copy-start.12
  141.4 1.5 copy-start.8
  251.8 1.7 copy-start.1
  251.8 1.7 copy-start.13
  251.8 2.8 copy-start.5
  253.5 1.6 copy-start.11
  253.8 0.8 copy-start.2
  255.3 6.1 collective-permute-start
  261.5 48.9 %collective-permute-start.1 = (f32[4096,128]{1,0:T(8,128)S(1)}, f32[4096,128]{1,0:T(8,128)S(1)}, u32[]{:S(2)}, u32[]{:S(2)}) collective-permute-start(f32[4096,128]{1,0:T(8,128)S(1)} %bitcast_add_fusion), channel_id=1, source_target_pairs={{0,2},{1,3},{2,0},{3,1},{4,6},{5,7},{6,4},{7,5},{8,10},{9,11},{10,... | collective-permute-start | bytes 6291464 | tf_op jit(solution)/shard_map/ppermute | solution.py:81
  310.6 95.2 %collective-permute-start.2 = (f32[4096,128]{1,0:T(8,128)S(1)}, f32[4096,128]{1,0:T(8,128)S(1)}, u32[]{:S(2)}, u32[]{:S(2)}) collective-permute-start(f32[4096,128]{1,0:T(8,128)S(1)} %add.85), channel_id=1, source_target_pairs={{0,4},{1,5},{2,6},{3,7},{4,0},{5,1},{6,2},{7,3},{8,12},{9,13},{10,... | collective-permute-start | bytes 6291464 | tf_op jit(solution)/shard_map/ppermute | solution.py:81
  406.1 97.0 %collective-permute-start.3 = (f32[4096,128]{1,0:T(8,128)S(1)}, f32[4096,128]{1,0:T(8,128)S(1)}, u32[]{:S(2)}, u32[]{:S(2)}) collective-permute-start(f32[4096,128]{1,0:T(8,128)S(1)} %add.86), channel_id=1, source_target_pairs={{0,8},{1,9},{2,10},{3,11},{4,12},{5,13},{6,14},{7,15},{8,0},{9,1},... | collective-permute-start | bytes 6291464 | tf_op jit(solution)/shard_map/ppermute | solution.py:81
  506.0 4.7 copy-start.10
  508.6 3.4 copy-start.3
Sparse Core Ops, SparseCore 0:
  12.2 104.7 all-gather.4
  119.1 96.7 all-gather.6
  504.8 215.0 reduce-scatter.1
